TPU v7x, 128 devices: a whole 4x4x4 slice. The times are simulated.
128 devices in a mesh: dp: 2 (over core), expert: 16 (over x, z), etp: 4 (over y).
Axes of the slice: x: 4, y: 4, z: 4, core: 2. Of those that a mesh axis runs over, the one named last changes fastest.
Arguments:
- master_old: float32 [16, 3584, 1024], P('expert', 'dp', 'etp'), may hold values from -6 to 6
- moment_old: float32 [16, 3584, 1024], P('expert', 'dp', 'etp'), may hold values from -6 to 6
- second_old: float32 [16, 3584, 1024], P('expert', 'dp', 'etp'), may hold values from 0.1 to 10
- grad_parts: bfloat16 [2, 32, 3584, 1024], P('dp', 'expert', None, 'etp'), may hold values from -384 to 384
- old_expert: int32 [16], replicated, may hold values from 0 to 15, as said below
- slot_expert: int32 [32], replicated, may hold values from -1 to 15, as said below
- owner_slot: int32 [16], replicated, may hold values from 0 to 31, as said below
- token_count: int32 [16], replicated, may hold values from 16 to 256
Outputs:
- master_new: float32 [32, 3584, 1024], P('expert', 'dp', 'etp')
- moment_new: float32 [32, 3584, 1024], P('expert', 'dp', 'etp')
- second_new: float32 [32, 3584, 1024], P('expert', 'dp', 'etp')
- slot_weights: bfloat16 [32, 3584, 1024], P('expert', None, 'etp')
Inputs may be any that keep to these rules, and one draw needn't show every extreme that they name: `old_expert`: every expert is named exactly once. `slot_expert`: every expert is hosted by one or two slots, never twice on one device; 4 experts have two. Slots s and s + 1 for even s belong to one device. Each device owns 0 to 2 experts, and some device owns exactly 2. Slot 0 and the last slot are owner slots. owner_slot[e] is a slot s with slot_expert[s] = e; each slot owns at most one expert.
All inputs are finite; a program needn't handle non-finite values.
Results may differ from a plain program's by a relative error of at most 0.009.
Values may be sent and summed in bfloat16 or wider, within the bound.
A program may use at most 128 MiB of HBM per device.

v0:
```python
import jax
import jax.numpy as jnp
from jax import lax
from jax.sharding import PartitionSpec as P

beta_one = 0.9
beta_two = 0.95
learn_rate = 0.05
decay_rate = 0.1
adam_eps = 1e-08


def for_sending(array):
    return jax.tree.map(lambda a: a.astype(jnp.bfloat16) if a.dtype == jnp.float32 else a, array)


def adamw_update(gradient, master, moment, second):
    moment_next = beta_one * moment + (1.0 - beta_one) * gradient
    second_next = beta_two * second + (1.0 - beta_two) * gradient * gradient
    master_next = master - learn_rate * (
        moment_next / (jnp.sqrt(second_next) + adam_eps) + decay_rate * master
    )
    return (master_next, moment_next, second_next)


def table_mix(mapping, stacked):
    leading = stacked.shape[0]
    flattened = stacked.reshape(leading, -1)
    mixed = jnp.dot(
        mapping, flattened, precision=lax.Precision.HIGHEST, preferred_element_type=jnp.float32
    )
    return mixed.reshape((mapping.shape[0],) + stacked.shape[1:])


def per_device(
    master_old, moment_old, second_old, grad_parts, old_expert, slot_expert, owner_slot, token_count
):
    expert_total = old_expert.shape[0]
    slot_total = slot_expert.shape[0]
    expert_ids = jnp.arange(expert_total, dtype=jnp.int32)
    slot_ids = jnp.arange(slot_total, dtype=jnp.int32)
    held_mask = slot_expert[:, None] == expert_ids[None, :]
    hold_map = held_mask.astype(jnp.float32)
    own_map = (held_mask & (owner_slot[None, :] == slot_ids[:, None])).astype(jnp.float32)
    from_old = (old_expert[None, :] == expert_ids[:, None]).astype(jnp.float32)
    counts = token_count.astype(jnp.float32)[:, None, None]
    halved = lax.psum_scatter(
        grad_parts[0].astype(jnp.float32).astype(jnp.bfloat16),
        "dp",
        scatter_dimension=1,
        tiled=True,
    ).astype(jnp.float32)
    master_piece = lax.all_to_all(
        master_old.astype(jnp.bfloat16), "expert", split_axis=1, concat_axis=0, tiled=True
    ).astype(master_old.dtype)
    moment_piece = lax.all_to_all(
        moment_old.astype(jnp.bfloat16), "expert", split_axis=1, concat_axis=0, tiled=True
    ).astype(moment_old.dtype)
    second_piece = lax.all_to_all(
        second_old.astype(jnp.bfloat16), "expert", split_axis=1, concat_axis=0, tiled=True
    ).astype(second_old.dtype)
    grad_piece = lax.all_to_all(
        halved.astype(jnp.bfloat16), "expert", split_axis=1, concat_axis=0, tiled=True
    ).astype(halved.dtype)
    gradient = table_mix(hold_map.T, grad_piece) / counts
    gathered = (
        gradient,
        table_mix(from_old, master_piece),
        table_mix(from_old, moment_piece),
        table_mix(from_old, second_piece),
    )
    gradient = lax.all_to_all(
        table_mix(own_map, gathered[0]).astype(jnp.bfloat16),
        "expert",
        split_axis=0,
        concat_axis=1,
        tiled=True,
    ).astype(jnp.float32)
    master = lax.all_to_all(
        table_mix(own_map, gathered[1]).astype(jnp.bfloat16),
        "expert",
        split_axis=0,
        concat_axis=1,
        tiled=True,
    ).astype(jnp.float32)
    moment = lax.all_to_all(
        table_mix(own_map, gathered[2]).astype(jnp.bfloat16),
        "expert",
        split_axis=0,
        concat_axis=1,
        tiled=True,
    ).astype(jnp.float32)
    second = lax.all_to_all(
        table_mix(own_map, gathered[3]).astype(jnp.bfloat16),
        "expert",
        split_axis=0,
        concat_axis=1,
        tiled=True,
    ).astype(jnp.float32)
    master_new, moment_new, second_new = adamw_update(gradient, master, moment, second)
    per_expert = table_mix(
        own_map.T,
        lax.all_to_all(
            for_sending(master_new), "expert", split_axis=1, concat_axis=0, tiled=True
        ).astype(master_new.dtype),
    )
    weights = table_mix(hold_map, per_expert).astype(jnp.bfloat16)
    weight_half = lax.all_to_all(weights, "expert", split_axis=0, concat_axis=1, tiled=True)
    slot_weights = lax.all_gather(weight_half, "dp", axis=1, tiled=True)
    return (master_new, moment_new, second_new, slot_weights)


def solution(mesh):
    placed = (
        P("expert", "dp", "etp"),
        P("expert", "dp", "etp"),
        P("expert", "dp", "etp"),
        P("dp", "expert", None, "etp"),
        P(),
        P(),
        P(),
        P(),
    )
    return jax.shard_map(
        per_device,
        mesh=mesh,
        in_specs=placed,
        out_specs=(
            P("expert", "dp", "etp"),
            P("expert", "dp", "etp"),
            P("expert", "dp", "etp"),
            P("expert", None, "etp"),
        ),
        check_vma=False,
    )
```

profile of v0, /device:TPU:1, one launch (start us, length us, event | category | flops | bytes accessed | tf_op | source)
XLA Modules:
  0.0 377.5 jit_solution(14060253880884209540)
XLA Ops:
  8.8 10.3 %copy.115 = bf16[1,1792,256]{2,0,1:T(2,128)(2,1)S(1)} copy(bf16[1,1792,256]{2,1,0:T(8,128)(2,1)S(1)} %convert_element_type.90) | data formatting | bytes 1835008 | tf_op jit(solution)/shard_map/convert_element_type | solution.py:54
  19.6 9.9 %reduce.6 = bf16[1792,256]{1,0:T(8,128)(2,1)S(1)} reduce(bf16[1792,1,256]{2,1,0:T(2,128)(2,1)S(1)} %bitcast.134, bf16[]{:T(256)} %broadcast.35), dimensions={1}, to_apply=%bitcast.116.reduce_sub_computation | reduce | bytes 1835010
  30.7 8.5 %all-to-all-start = ((bf16[16,2,14336]{2,1,0:T(2,128)(2,1)}), bf16[16,2,14336]{2,1,0:T(2,128)(2,1)}, u32[]{:S(2)}, u32[]{:S(2)}) async-start(bf16[16,2,14336]{2,1,0:T(2,128)(2,1)} %reshape.92), calls=%async_computation | async-start | bytes 1835008 | tf_op jit(solution)/shard_map/all_to_all | solution.py:53
  39.2 10.3 %copy.114 = bf16[1,1792,256]{2,0,1:T(2,128)(2,1)S(1)} copy(bf16[1,1792,256]{2,1,0:T(8,128)(2,1)S(1)} %convert_element_type.97) | data formatting | bytes 1835008 | tf_op jit(solution)/shard_map/convert_element_type | solution.py:57
  49.5 9.9 %reduce.8 = bf16[1792,256]{1,0:T(8,128)(2,1)S(1)} reduce(bf16[1792,1,256]{2,1,0:T(2,128)(2,1)S(1)} %bitcast.136, bf16[]{:T(256)} %broadcast.35), dimensions={1}, to_apply=%bitcast.115.reduce_sub_computation | reduce | bytes 1835010
  60.6 6.7 %all-to-all-start.2 = ((bf16[16,2,14336]{2,1,0:T(2,128)(2,1)}), bf16[16,2,14336]{2,1,0:T(2,128)(2,1)}, u32[]{:S(2)}, u32[]{:S(2)}) async-start(bf16[16,2,14336]{2,1,0:T(2,128)(2,1)} %reshape.94), calls=%async_computation.2 | async-start | bytes 1835008 | tf_op jit(solution)/shard_map/all_to_all | solution.py:56
  67.5 9.1 %copy.112 = bf16[1,2,3584,256]{3,1,2,0:T(2,128)(2,1)} copy(bf16[1,2,3584,256]{3,2,1,0:T(8,128)(2,1)} %param.11) | data formatting | bytes 7340032 | tf_op args[3]
  78.2 10.3 %copy.113 = bf16[1,1792,256]{2,0,1:T(2,128)(2,1)S(1)} copy(bf16[1,1792,256]{2,1,0:T(8,128)(2,1)S(1)} %convert_element_type.107) | data formatting | bytes 1835008 | tf_op jit(solution)/shard_map/convert_element_type | solution.py:60
  88.5 9.9 %reduce.7 = bf16[1792,256]{1,0:T(8,128)(2,1)S(1)} reduce(bf16[1792,1,256]{2,1,0:T(2,128)(2,1)S(1)} %bitcast.135, bf16[]{:T(256)} %broadcast.35), dimensions={1}, to_apply=%bitcast.114.reduce_sub_computation | reduce | bytes 1835010
  99.6 4.2 %reshape.93 = bf16[1792,1,256]{2,1,0:T(2,128)(2,1)S(1)} reshape(bf16[16,2,14336]{2,1,0:T(2,128)(2,1)} %all-to-all-done) | data formatting | bytes 1835008
  103.8 6.6 %all-to-all-start.6 = ((bf16[16,2,14336]{2,1,0:T(2,128)(2,1)}), bf16[16,2,14336]{2,1,0:T(2,128)(2,1)S(1)}, u32[]{:S(2)}, u32[]{:S(2)}) async-start(bf16[16,2,14336]{2,1,0:T(2,128)(2,1)} %reshape.96), calls=%async_computation.6 | async-start | bytes 1835008 | tf_op jit(solution)/shard_map/all_to_all | solution.py:59
  110.5 10.6 %bitcast_reduce_fusion.2 = bf16[1792,256]{1,0:T(8,128)(2,1)} fusion(bf16[1792,1,256]{2,1,0:T(2,128)(2,1)S(1)} %reshape.93), kind=kLoop, calls=%fused_computation.43 | loop fusion | bytes 1835008 | tf_op jit(solution)/shard_map/all_to_all | solution.py:53
  127.6 7.1 %all-to-all-start.1 = ((bf16[32,112,256]{2,1,0:T(8,128)(2,1)}), bf16[32,112,256]{2,1,0:T(8,128)(2,1)S(1)}, u32[]{:S(2)}, u32[]{:S(2)}) async-start(bf16[32,112,256]{2,1,0:T(8,128)(2,1)} %bitcast.38), calls=%async_computation.1 | async-start | bytes 3670016 | tf_op jit(solution)/shard_map/all_to_all | solution.py:79
  134.7 5.6 %reshape.95 = bf16[1792,1,256]{2,1,0:T(2,128)(2,1)} reshape(bf16[16,2,14336]{2,1,0:T(2,128)(2,1)} %all-to-all-done.2) | data formatting | bytes 1835008
  140.3 11.6 %bitcast_reduce_fusion.1 = bf16[1792,256]{1,0:T(8,128)(2,1)} fusion(bf16[1792,1,256]{2,1,0:T(2,128)(2,1)} %reshape.95), kind=kLoop, calls=%fused_computation.42 | loop fusion | bytes 1835008 | tf_op jit(solution)/shard_map/all_to_all | solution.py:56
  158.8 6.5 %all-to-all-start.3 = ((bf16[32,112,256]{2,1,0:T(8,128)(2,1)}), bf16[32,112,256]{2,1,0:T(8,128)(2,1)}, u32[]{:S(2)}, u32[]{:S(2)}) async-start(bf16[32,112,256]{2,1,0:T(8,128)(2,1)} %bitcast.40), calls=%async_computation.3 | async-start | bytes 3670016 | tf_op jit(solution)/shard_map/all_to_all | solution.py:86
  166.6 4.1 %constant_dynamic-slice_fusion = bf16[2,1792,256]{2,0,1:T(2,128)(2,1)} fusion(bf16[2,3584,256]{2,0,1:T(2,128)(2,1)} %all-reduce.3.cloned.1.call-done, u32[]{:T(128)S(6)} %multiply.1), kind=kLoop, calls=%fused_computation.38 | loop fusion | bytes 3670020
  170.6 17.3 %all-to-all-done.3 = bf16[32,112,256]{2,1,0:T(8,128)(2,1)} async-done(((bf16[32,112,256]{2,1,0:T(8,128)(2,1)}), bf16[32,112,256]{2,1,0:T(8,128)(2,1)}, u32[]{:S(2)}, u32[]{:S(2)}) %all-to-all-start.3) | async-done | bytes 1835040 | tf_op jit(solution)/shard_map/all_to_all | solution.py:86
  187.9 5.4 %all-to-all-start.4 = ((bf16[2,1792,256]{2,0,1:T(2,128)(2,1)}), bf16[2,1792,256]{2,0,1:T(2,128)(2,1)S(1)}, u32[]{:S(2)}, u32[]{:S(2)}) async-start(bf16[2,1792,256]{2,0,1:T(2,128)(2,1)} %constant_dynamic-slice_fusion), calls=%async_computation.4 | async-start | bytes 3670016 | tf_op jit(solution)/shard_map/all_to_all | solution.py:62
  196.7 11.6 %bitcast_reduce_fusion = bf16[1792,256]{1,0:T(8,128)(2,1)} fusion(bf16[1792,1,256]{2,1,0:T(2,128)(2,1)} %reshape.97), kind=kLoop, calls=%fused_computation.41 | loop fusion | bytes 1835008 | tf_op jit(solution)/shard_map/all_to_all | solution.py:59
  214.4 7.6 %all-to-all-start.7 = ((bf16[32,112,256]{2,1,0:T(8,128)(2,1)}), bf16[32,112,256]{2,1,0:T(8,128)(2,1)}, u32[]{:S(2)}, u32[]{:S(2)}) async-start(bf16[32,112,256]{2,1,0:T(8,128)(2,1)} %bitcast.121), calls=%async_computation.7 | async-start | bytes 3670016 | tf_op jit(solution)/shard_map/all_to_all | solution.py:93
  227.0 17.6 %all-to-all-done.7 = bf16[32,112,256]{2,1,0:T(8,128)(2,1)} async-done(((bf16[32,112,256]{2,1,0:T(8,128)(2,1)}), bf16[32,112,256]{2,1,0:T(8,128)(2,1)}, u32[]{:S(2)}, u32[]{:S(2)}) %all-to-all-start.7) | async-done | bytes 1835040 | tf_op jit(solution)/shard_map/all_to_all | solution.py:93
  244.6 5.0 %all-to-all-start.5 = ((bf16[32,112,256]{2,1,0:T(8,128)(2,1)}), bf16[32,112,256]{2,1,0:T(8,128)(2,1)S(1)}, u32[]{:S(2)}, u32[]{:S(2)}) async-start(bf16[32,112,256]{2,1,0:T(8,128)(2,1)} %copy.72), calls=%async_computation.5 | async-start | bytes 3670016 | tf_op jit(solution)/shard_map/all_to_all | solution.py:72
  251.8 4.7 %copy.75 = f32[16,2,112,256]{3,1,2,0:T(2,128)} copy(f32[16,2,112,256]{3,2,1,0:T(8,128)S(1)} %bitcast.118) | data formatting | bytes 7340032 | tf_op jit(solution)/shard_map/mul | solution.py:19
  258.5 4.7 %copy.66 = f32[16,2,112,256]{3,1,2,0:T(2,128)} copy(f32[16,2,112,256]{3,2,1,0:T(8,128)S(1)} %bitcast.119) | data formatting | bytes 7340032 | tf_op jit(solution)/shard_map/mul | solution.py:18
  266.4 4.2 %all-to-all-done.5 = bf16[32,112,256]{2,1,0:T(8,128)(2,1)S(1)} async-done(((bf16[32,112,256]{2,1,0:T(8,128)(2,1)}), bf16[32,112,256]{2,1,0:T(8,128)(2,1)S(1)}, u32[]{:S(2)}, u32[]{:S(2)}) %all-to-all-start.5) | async-done | bytes 1835040 | tf_op jit(solution)/shard_map/all_to_all | solution.py:72
  275.0 12.6 %fusion.32 = (bf16[2,1792,256]{2,0,1:T(2,128)(2,1)S(1)}, f32[2,1792,256]{2,0,1:T(2,128)}, f32[2,1792,256]{2,0,1:T(2,128)}, f32[2,1792,256]{2,0,1:T(2,128)}) fusion(f32[16,2,112,256]{3,1,2,0:T(2,128)S(1)} %copy-done.4, f32[2,16,112,256]{3,0,2,1:T(2,128)S(1)} %copy.73, f32[16,2,112,256]{3,1,2,0:T(2,128)S(1)} %copy-done.2, f32[16,2,112,256]{3,1,2,0:T(2,128)S(1)} %copy-done.3), kind=kLoop, calls=%fused_computation.40 | loop fusion | flops 11010048 | bytes 27525120 | tf_op jit(solution)/shard_map/convert_element_type | solution.py:14
  287.6 30.0 %all_to_all.111 = bf16[2,1792,256]{2,0,1:T(2,128)(2,1)S(1)} all-to-all(bf16[2,1792,256]{2,0,1:T(2,128)(2,1)S(1)} %get-tuple-element.16), channel_id=1, replica_groups=mesh['dp'=2,'expert'=16,'etp'=4] {'expert'}, dimensions={1} | all-to-all | bytes 3670016 | tf_op jit(solution)/shard_map/all_to_all | solution.py:103
  321.1 25.2 %all_to_all.112 = bf16[32,112,256]{2,1,0:T(8,128)(2,1)S(1)} all-to-all(bf16[32,112,256]{2,1,0:T(8,128)(2,1)S(1)} %bitcast.125), channel_id=1, replica_groups=mesh['dp'=2,'expert'=16,'etp'=4] {'expert'}, dimensions={0} | all-to-all | bytes 3670016 | tf_op jit(solution)/shard_map/all_to_all | solution.py:108
  347.7 4.3 %copy.78 = f32[2,1792,256]{2,1,0:T(8,128)} copy(f32[2,1792,256]{2,0,1:T(2,128)} %get-tuple-element.17) | data formatting | bytes 7340032
  357.5 8.5 %all-gather.2.cloned.1.call-done = bf16[2,3584,256]{2,1,0:T(8,128)(2,1)} async-done(((bf16[2,1792,256]{2,1,0:T(8,128)(2,1)}), bf16[2,3584,256]{2,1,0:T(8,128)(2,1)}) %all-gather.2.cloned.1.call-update) | async-done | bytes 3670032 | tf_op jit(solution)/shard_map/all_gather | solution.py:109
  366.1 4.1 %copy.118 = bf16[2,3584,256]{2,1,0:T(8,128)(2,1)} copy(bf16[2,3584,256]{2,1,0:T(8,128)(2,1)} %all-gather.2.cloned.1.call-done) | data formatting | bytes 7340032
  (81 shorter events, 57.8 us)
Async XLA Ops:
  29.5 9.6 %copy-start.9 = (f32[1,1792,256]{2,1,0:T(8,128)S(1)}, f32[1,1792,256]{2,1,0:T(8,128)}, u32[]{:S(2)}) copy-start(f32[1,1792,256]{2,1,0:T(8,128)} %param.9) | copy-start | bytes 5505028
  30.7 30.0 %all-to-all-start = ((bf16[16,2,14336]{2,1,0:T(2,128)(2,1)}), bf16[16,2,14336]{2,1,0:T(2,128)(2,1)}, u32[]{:S(2)}, u32[]{:S(2)}) async-start(bf16[16,2,14336]{2,1,0:T(2,128)(2,1)} %reshape.92), calls=%async_computation | async-start | bytes 1835008 | tf_op jit(solution)/shard_map/all_to_all | solution.py:53
  60.6 43.2 %all-to-all-start.2 = ((bf16[16,2,14336]{2,1,0:T(2,128)(2,1)}), bf16[16,2,14336]{2,1,0:T(2,128)(2,1)}, u32[]{:S(2)}, u32[]{:S(2)}) async-start(bf16[16,2,14336]{2,1,0:T(2,128)(2,1)} %reshape.94), calls=%async_computation.2 | async-start | bytes 1835008 | tf_op jit(solution)/shard_map/all_to_all | solution.py:56
  67.3 99.3 %all-reduce.3.cloned.1.call-start = ((), (), s32[]{:S(2)}) async-start(), calls=%async_computation.11 | async-start | bytes 7340032
  76.6 1.5 copy-start.10
  103.8 22.8 %all-to-all-start.6 = ((bf16[16,2,14336]{2,1,0:T(2,128)(2,1)}), bf16[16,2,14336]{2,1,0:T(2,128)(2,1)S(1)}, u32[]{:S(2)}, u32[]{:S(2)}) async-start(bf16[16,2,14336]{2,1,0:T(2,128)(2,1)} %reshape.96), calls=%async_computation.6 | async-start | bytes 1835008 | tf_op jit(solution)/shard_map/all_to_all | solution.py:59
  110.5 12.2 %copy-start.13 = (s32[16]{0:T(128)S(1)}, s32[16]{0:T(128)}, u32[]{:S(2)}) copy-start(s32[16]{0:T(128)} %param.12) | copy-start | bytes 196
  122.7 0.7 copy-start.11
  122.7 0.7 copy-start.12
  126.7 0.9 copy-start.7
  127.6 30.0 %all-to-all-start.1 = ((bf16[32,112,256]{2,1,0:T(8,128)(2,1)}), bf16[32,112,256]{2,1,0:T(8,128)(2,1)S(1)}, u32[]{:S(2)}, u32[]{:S(2)}) async-start(bf16[32,112,256]{2,1,0:T(8,128)(2,1)} %bitcast.38), calls=%async_computation.1 | async-start | bytes 3670016 | tf_op jit(solution)/shard_map/all_to_all | solution.py:79
  157.6 1.2 copy-start.5
  157.6 7.7 %copy-start.15 = (u32[128]{0:T(128)S(1)}, u32[128]{0:T(128)}, u32[]{:S(2)}) copy-start(u32[128]{0:T(128)} %constant.16) | copy-start | bytes 1540
  158.8 29.1 %all-to-all-start.3 = ((bf16[32,112,256]{2,1,0:T(8,128)(2,1)}), bf16[32,112,256]{2,1,0:T(8,128)(2,1)}, u32[]{:S(2)}, u32[]{:S(2)}) async-start(bf16[32,112,256]{2,1,0:T(8,128)(2,1)} %bitcast.40), calls=%async_computation.3 | async-start | bytes 3670016 | tf_op jit(solution)/shard_map/all_to_all | solution.py:86
  170.6 22.7 %copy-start.8 = (bf16[16,2,14336]{2,1,0:T(2,128)(2,1)S(1)}, bf16[16,2,14336]{2,1,0:T(2,128)(2,1)}, u32[]{:S(2)}) copy-start(bf16[16,2,14336]{2,1,0:T(2,128)(2,1)} %copy-done.7) | copy-start | bytes 2752516
  187.9 26.4 %all-to-all-start.4 = ((bf16[2,1792,256]{2,0,1:T(2,128)(2,1)}), bf16[2,1792,256]{2,0,1:T(2,128)(2,1)S(1)}, u32[]{:S(2)}, u32[]{:S(2)}) async-start(bf16[2,1792,256]{2,0,1:T(2,128)(2,1)} %constant_dynamic-slice_fusion), calls=%async_computation.4 | async-start | bytes 3670016 | tf_op jit(solution)/shard_map/all_to_all | solution.py:62
  214.4 7.6 %copy-start.14 = (s32[16]{0:T(128)S(1)}, s32[16]{0:T(128)}, u32[]{:S(2)}) copy-start(s32[16]{0:T(128)} %param.15) | copy-start | bytes 196
  214.4 30.2 %all-to-all-start.7 = ((bf16[32,112,256]{2,1,0:T(8,128)(2,1)}), bf16[32,112,256]{2,1,0:T(8,128)(2,1)}, u32[]{:S(2)}, u32[]{:S(2)}) async-start(bf16[32,112,256]{2,1,0:T(8,128)(2,1)} %bitcast.121), calls=%async_computation.7 | async-start | bytes 3670016 | tf_op jit(solution)/shard_map/all_to_all | solution.py:93
  244.6 26.1 %all-to-all-start.5 = ((bf16[32,112,256]{2,1,0:T(8,128)(2,1)}), bf16[32,112,256]{2,1,0:T(8,128)(2,1)S(1)}, u32[]{:S(2)}, u32[]{:S(2)}) async-start(bf16[32,112,256]{2,1,0:T(8,128)(2,1)} %copy.72), calls=%async_computation.5 | async-start | bytes 3670016 | tf_op jit(solution)/shard_map/all_to_all | solution.py:72
  249.6 116.5 %all-gather.2.cloned.1.call-start = ((), (), s32[]{:S(2)}) async-start(), calls=%async_computation.10 | async-start | bytes 5505024 | tf_op jit(solution)/shard_map/all_gather | solution.py:109
  258.5 4.7 %copy-start.6 = (bf16[32,112,256]{2,1,0:T(8,128)(2,1)S(1)}, bf16[32,112,256]{2,1,0:T(8,128)(2,1)}, u32[]{:S(2)}) copy-start(bf16[32,112,256]{2,1,0:T(8,128)(2,1)} %copy-done.5) | copy-start | bytes 5505028
  270.7 3.3 copy-start.4
  271.1 2.9 copy-start.2
  271.1 3.9 %copy-start.3 = (f32[16,2,112,256]{3,1,2,0:T(2,128)S(1)}, f32[16,2,112,256]{3,1,2,0:T(2,128)}, u32[]{:S(2)}) copy-start(f32[16,2,112,256]{3,1,2,0:T(2,128)} %copy.66) | copy-start | bytes 11010052
  347.7 4.3 %copy-start.1 = (f32[2,1792,256]{2,0,1:T(2,128)S(1)}, f32[2,1792,256]{2,0,1:T(2,128)}, u32[]{:S(2)}) copy-start(f32[2,1792,256]{2,0,1:T(2,128)} %get-tuple-element.18) | copy-start | bytes 11010052
  352.0 3.4 copy-start
Sparse Core Ops, SparseCore 0:
  76.8 32.8 all-reduce.2
  347.8 18.1 all-gather.1
where the time goes:
time: 385 us; the launch traced here: 377 us
  local copies, waits for them, and re-layouts  145 us (38%)
  blocking collectives  55.2 us (14%)
  starting transfers between devices  53.8 us (14%)
  waiting for transfers between devices  48.8 us (13%)
  other arithmetic  48.6 us (13%)
  between operations  15.5 us (4%)
  matrix products  10.8 us (3%)
    unnamed x51, local copies, waits for them, and re-layouts  55.4 us
    all_to_all x1, blocking collectives, per_device(): lax.all_to_all(for_sending(master_new), 'expert', split_axis=1, concat_ax...  30 us
    unnamed x3, other arithmetic  29.8 us
    all_to_all x1, blocking collectives, per_device(): lax.all_to_all(weights, 'expert', split_axis=0, concat_axis=1, tiled=True)  25.2 us
    all_to_all x1, waiting for transfers between devices, per_device(): lax.all_to_all(table_mix(own_map, gathered[3]).astype(jnp.bfloat16), 'exp...  17.6 us
    all_to_all x1, waiting for transfers between devices, per_device(): lax.all_to_all(table_mix(own_map, gathered[2]).astype(jnp.bfloat16), 'exp...  17.3 us
    convert_element_type x1, other arithmetic, for_sending(): a.astype(jnp.bfloat16)  12.6 us
    all_to_all x1, local copies, waits for them, and re-layouts, per_device(): lax.all_to_all(moment_old.astype(jnp.bfloat16), 'expert', split_axis=1, c...  11.6 us
  transfers between devices with their start and end apart: 10, of which 6 were waited for; matrix products, arithmetic and copies ran while one was open for 40% of the time, Pallas kernels for 0%

commit v1 on v0

v1 whole, which is shorter than its diff:
```python
import functools

import jax
import jax.numpy as jnp
from jax import lax
from jax.experimental import pallas as pl
from jax.experimental.pallas import tpu as pltpu
from jax.sharding import PartitionSpec as P

beta_one = 0.9
beta_two = 0.95
learn_rate = 0.05
decay_rate = 0.1
adam_eps = 1e-08

MESH = pl.DeviceIdType.MESH
SIDE = 4
PEERS = SIDE * SIDE
FIELDS = 5
RESULTS = 6
PIECE = 16
ORDER = (
    (0, 1), (0, 3), (1, 0), (3, 0), (1, 1), (3, 3), (1, 3), (3, 1),
    (0, 2), (2, 0), (2, 1), (2, 3), (1, 2), (3, 2), (2, 2),
)


def exchange_kernel(
    chunks,
    old_ref, slot_ref, count_ref,
    master_ref, moment_ref, second_ref, grad_ref,
    out_ref, other_ref,
    *scratch,
):
    landed = scratch[:chunks]
    (states, grad_own, grad_other, packed, updated, table,
     load_sem, dp_send, dp_recv, send_one, recv_one, send_two, recv_two,
     fwd_send, fwd_recv) = scratch[chunks:]
    rows = states.shape[2]
    half = chunks * rows
    core = lax.axis_index("dp")
    me = lax.axis_index("expert")
    plane = lax.axis_index("etp")
    my_x = me // SIDE
    my_z = me % SIDE
    partner = (1 - core, me, plane)
    targets = [
        lax.rem(my_x + dx, SIDE) * SIDE + lax.rem(my_z + dz, SIDE) for dx, dz in ORDER
    ]

    def loads(k):
        window = pl.ds(k * rows, rows)
        copies = [
            pltpu.make_async_copy(ref.at[0, window], states.at[k, a], load_sem.at[k, a])
            for a, ref in enumerate((master_ref, moment_ref, second_ref))
        ]
        copies.append(
            pltpu.make_async_copy(
                grad_ref.at[0, :, pl.ds(core * half + k * rows, rows)],
                grad_own.at[k],
                load_sem.at[k, 3],
            )
        )
        return copies

    def swap(k):
        return pltpu.make_async_remote_copy(
            src_ref=grad_ref.at[0, :, pl.ds((1 - core) * half + k * rows, rows)],
            dst_ref=grad_other.at[k],
            send_sem=dp_send.at[k],
            recv_sem=dp_recv.at[k],
            device_id=partner,
            device_id_type=MESH,
        )

    def scatter(k):
        for other in targets:
            pltpu.make_async_remote_copy(
                src_ref=packed.at[k, other],
                dst_ref=landed[k].at[pl.ds(me * FIELDS, FIELDS)],
                send_sem=send_one.at[k],
                recv_sem=recv_one.at[k],
                device_id=(core, other, plane),
                device_id_type=MESH,
            ).start()
        pltpu.make_async_copy(
            packed.at[k, me], landed[k].at[pl.ds(me * FIELDS, FIELDS)], recv_one.at[k]
        ).start()

    def deliver(k):
        window = pl.ds(k * rows + me * PIECE, PIECE)
        for other in targets:
            pltpu.make_async_remote_copy(
                src_ref=updated.at[k, other],
                dst_ref=out_ref.at[:, window],
                send_sem=send_two.at[k],
                recv_sem=recv_two.at[k],
                device_id=(core, other, plane),
                device_id_type=MESH,
            ).start()
        pltpu.make_async_copy(
            updated.at[k, me], out_ref.at[:, window], recv_two.at[k]
        ).start()

    def pack(k):
        for copy in loads(k):
            copy.wait()
        swap(k).wait_recv()

        def body(i, carry):
            window = pl.ds(pl.multiple_of(i * PIECE, PIECE), PIECE)
            for a in range(3):
                packed[k, i, a] = states[k, a, window].astype(jnp.bfloat16)
            for h in range(2):
                packed[k, i, 3 + h] = (
                    grad_own[k, h, window].astype(jnp.float32)
                    + grad_other[k, h, window].astype(jnp.float32)
                ).astype(jnp.bfloat16)
            return carry

        lax.fori_loop(0, PEERS, body, 0)

    def update(k):
        source = landed[k]

        def body(d, carry):
            for h in range(2):
                s = 2 * d + h
                state = table[0, s]
                first = table[1, s]
                last = table[2, s]
                twice = table[3, s].astype(jnp.float32)
                scale = 1.0 / jnp.full((PIECE, 256), table[4, s].astype(jnp.float32))
                gradient = (
                    source[first].astype(jnp.float32)
                    + twice * source[last].astype(jnp.float32)
                ) * scale
                master = source[state].astype(jnp.float32)
                moment = source[state + 1].astype(jnp.float32)
                second = source[state + 2].astype(jnp.float32)
                moment = beta_one * moment + (1.0 - beta_one) * gradient
                second = beta_two * second + (1.0 - beta_two) * gradient * gradient
                master = master - learn_rate * (
                    moment / (jnp.sqrt(second) + adam_eps) + decay_rate * master
                )
                updated[k, d, h] = master.astype(jnp.bfloat16)
                updated[k, d, 2 + h] = moment.astype(jnp.bfloat16)
                updated[k, d, 4 + h] = second.astype(jnp.bfloat16)
            return carry

        lax.fori_loop(0, PEERS, body, 0)

    def forward(k):
        window = pl.ds(k * rows, rows)
        return pltpu.make_async_remote_copy(
            src_ref=out_ref.at[pl.ds(0, 2), window],
            dst_ref=other_ref.at[:, window],
            send_sem=fwd_send.at[k],
            recv_sem=fwd_recv.at[k],
            device_id=partner,
            device_id_type=MESH,
        )

    def all_bytes(ref, sem):
        pltpu.make_async_copy(ref, ref, sem).wait()

    for k in range(chunks):
        for copy in loads(k):
            copy.start()

    barrier = pltpu.get_barrier_semaphore()
    for other in targets:
        pl.semaphore_signal(
            barrier, inc=1, device_id=(core, other, plane), device_id_type=MESH
        )
    pl.semaphore_signal(barrier, inc=1, device_id=partner, device_id_type=MESH)
    pl.semaphore_wait(barrier, PEERS)

    for k in range(chunks):
        swap(k).start()

    def fill_table(s, carry):
        expert = jnp.maximum(slot_ref[s], 0)
        holder = jnp.int32(0)
        for j in range(PEERS):
            holder = jnp.where(old_ref[j] == expert, j, holder)
        first = jnp.int32(0)
        last = jnp.int32(0)
        for t in range(2 * PEERS):
            last = jnp.where(slot_ref[t] == expert, t, last)
            back = 2 * PEERS - 1 - t
            first = jnp.where(slot_ref[back] == expert, back, first)
        table[0, s] = holder * FIELDS
        table[1, s] = (first // 2) * FIELDS + 3 + first % 2
        table[2, s] = (last // 2) * FIELDS + 3 + last % 2
        table[3, s] = jnp.where(first == last, 0, 1)
        table[4, s] = count_ref[expert]
        return carry

    pack(0)
    scatter(0)
    pack(1)
    scatter(1)
    lax.fori_loop(0, 2 * PEERS, fill_table, 0)
    for k in range(chunks):
        all_bytes(landed[k], recv_one.at[k])
        update(k)
        deliver(k)
        if k + 2 < chunks:
            pack(k + 2)
            scatter(k + 2)
    for k in range(chunks):
        all_bytes(out_ref.at[:, pl.ds(k * rows, rows)], recv_two.at[k])
        forward(k).start()
    for k in range(chunks):
        swap(k).wait_send()
        all_bytes(packed.at[k, pl.ds(0, PEERS - 1)], send_one.at[k])
        all_bytes(updated.at[k, pl.ds(0, PEERS - 1)], send_two.at[k])
    for k in range(chunks):
        forward(k).wait()


def expand_kernel(slot_ref, owner_ref, here_ref, there_ref, master_ref, moment_ref, second_ref, weight_ref):
    core = lax.axis_index("dp")
    me = lax.axis_index("expert")
    for h in range(2):
        slot = 2 * me + h
        expert = slot_ref[slot]
        held = expert >= 0
        owned = held & (owner_ref[jnp.maximum(expert, 0)] == slot)
        master = here_ref[h]
        for ref, field in ((master_ref, 0), (moment_ref, 2), (second_ref, 4)):
            value = here_ref[field + h].astype(jnp.float32)
            ref[h] = jnp.where(owned, value, 0.0)
        here = jnp.where(held, master.astype(jnp.float32), 0.0).astype(jnp.bfloat16)
        there = jnp.where(held, there_ref[h].astype(jnp.float32), 0.0).astype(jnp.bfloat16)
        weight_ref[h, core] = here
        weight_ref[h, 1 - core] = there


def per_device(
    master_old, moment_old, second_old, grad_parts, old_expert, slot_expert, owner_slot, token_count
):
    half, width = master_old.shape[1:]
    rows = PEERS * PIECE
    chunks = half // rows
    anywhere = pl.BlockSpec(memory_space=pl.ANY)
    scalars = pl.BlockSpec(memory_space=pltpu.SMEM)
    bf16 = jnp.bfloat16
    dma = pltpu.SemaphoreType.DMA
    here, there = pl.pallas_call(
        functools.partial(exchange_kernel, chunks),
        out_shape=(
            jax.ShapeDtypeStruct((RESULTS, half, width), bf16),
            jax.ShapeDtypeStruct((2, half, width), bf16),
        ),
        in_specs=[scalars] * 3 + [anywhere] * 4,
        out_specs=(anywhere, anywhere),
        scratch_shapes=[pltpu.VMEM((PEERS * FIELDS, PIECE, width), bf16)] * chunks
        + [
            pltpu.VMEM((chunks, 3, rows, width), jnp.float32),
            pltpu.VMEM((chunks, 2, rows, width), bf16),
            pltpu.VMEM((chunks, 2, rows, width), bf16),
            pltpu.VMEM((chunks, PEERS, FIELDS, PIECE, width), bf16),
            pltpu.VMEM((chunks, PEERS, RESULTS, PIECE, width), bf16),
            pltpu.SMEM((5, 2 * PEERS), jnp.int32),
            dma((chunks, 4)),
        ]
        + [dma((chunks,))] * 8,
        compiler_params=pltpu.CompilerParams(collective_id=0, has_side_effects=True),
        name="exchange",
    )(old_expert, slot_expert, token_count, master_old, moment_old, second_old, grad_parts)

    block = 256
    wide = jax.ShapeDtypeStruct((2, half, width), jnp.float32)
    state_spec = pl.BlockSpec((2, block, width), lambda i: (0, i, 0))
    master_new, moment_new, second_new, weights = pl.pallas_call(
        expand_kernel,
        out_shape=(wide, wide, wide, jax.ShapeDtypeStruct((2, 2, half, width), bf16)),
        grid=(half // block,),
        in_specs=[
            scalars,
            scalars,
            pl.BlockSpec((RESULTS, block, width), lambda i: (0, i, 0)),
            state_spec,
        ],
        out_specs=(
            state_spec,
            state_spec,
            state_spec,
            pl.BlockSpec((2, 2, block, width), lambda i: (0, 0, i, 0)),
        ),
        name="expand",
    )(slot_expert, owner_slot, here, there)
    return (master_new, moment_new, second_new, weights.reshape(2, 2 * half, width))


def solution(mesh):
    placed = (
        P("expert", "dp", "etp"),
        P("expert", "dp", "etp"),
        P("expert", "dp", "etp"),
        P("dp", "expert", None, "etp"),
        P(),
        P(),
        P(),
        P(),
    )
    return jax.shard_map(
        per_device,
        mesh=mesh,
        in_specs=placed,
        out_specs=(
            P("expert", "dp", "etp"),
            P("expert", "dp", "etp"),
            P("expert", "dp", "etp"),
            P("expert", None, "etp"),
        ),
        check_vma=False,
    )
```

time: 385 us -> 135 us (0.35); the launches traced: 377 us -> 134 us
  local copies, waits for them, and re-layouts: 145 us -> 0 us
  Pallas kernels: 0 us -> 134 us
  blocking collectives: 55.2 us -> 0 us
  starting transfers between devices: 53.8 us -> 0 us
  waiting for transfers between devices: 48.8 us -> 0 us
  other arithmetic: 48.6 us -> 0 us
  between operations: 15.5 us -> 0.64 us
  matrix products: 10.8 us -> 0 us
    pallas_call x0 -> x2, Pallas kernels: none -> 134 us  [the longest x1 124 us: per_device(): pl.pallas_call(functools.partial(exchange_kernel, chunks), out_shape=(jax...]
    unnamed x51 -> x0, local copies, waits for them, and re-layouts: 55.4 us -> none
    all_to_all x2 -> x0, blocking collectives: 55.2 us -> none  [the longest x1 30 us: per_device(): lax.all_to_all(for_sending(master_new), 'expert', split_axis=1, concat_ax...]
    all_to_all x8 -> x0, starting transfers between devices: 53.3 us -> none  [the longest x1 8.46 us: per_device(): lax.all_to_all(master_old.astype(jnp.bfloat16), 'expert', split_axis=1, c...]
    all_to_all x8 -> x0, waiting for transfers between devices: 40.2 us -> none  [the longest x1 17.6 us: per_device(): lax.all_to_all(table_mix(own_map, gathered[3]).astype(jnp.bfloat16), 'exp...]
    convert_element_type x6 -> x0, local copies, waits for them, and re-layouts: 39.3 us -> none  [the longest x1 10.3 us: per_device(): master_old.astype(jnp.bfloat16)]
    all_to_all x6 -> x0, local copies, waits for them, and re-layouts: 35.8 us -> none  [the longest x1 11.6 us: per_device(): lax.all_to_all(moment_old.astype(jnp.bfloat16), 'expert', split_axis=1, c...]
    unnamed x3 -> x0, other arithmetic: 29.8 us -> none
  transfers between devices with their start and end apart: 10 -> 0, of which waited for: 6 -> 0; matrix products, arithmetic and copies ran while one was open for 40% -> 0% of each run, Pallas kernels for 0% -> 0%
where the time goes in v1:
time: 135 us; the launch traced here: 134 us
  Pallas kernels  134 us (99%)
    pallas_call x1, Pallas kernels, per_device(): pl.pallas_call(functools.partial(exchange_kernel, chunks), out_shape=(jax...  124 us
    pallas_call x1, Pallas kernels, per_device(): pl.pallas_call(expand_kernel, out_shape=(wide, wide, wide, jax.ShapeDtype...  9.39 us

profile of v1, /device:TPU:1, one launch (start us, length us, event | category | flops | bytes accessed | tf_op | source)
XLA Modules:
  0.0 134.2 jit_solution(6563328373693986915)
XLA Ops:
  0.6 124.2 %exchange.1 = (bf16[6,1792,256]{2,1,0:T(8,128)(2,1)}, bf16[2,1792,256]{2,1,0:T(8,128)(2,1)}) custom-call(s32[16]{0:T(128)} %old_ref.1, s32[32]{0:T(128)} %slot_ref.3, s32[16]{0:T(128)} %count_ref.1, f32[1,1792,256]{2,1,0:T(8,128)} %master_ref.1, f32[1,1792,256]{2,1,0:T(8,128)} %moment_ref.1, f32[1,1792,256]{2,1,0:T(8,128)} %second_ref.1, ...), custom_call_target="tpu_custom_call" | custom-call | tf_op jit(solution)/shard_map/exchange/pallas_call | solution.py:251
  124.8 9.4 %expand.1 = (f32[2,1792,256]{2,1,0:T(8,128)}, f32[2,1792,256]{2,1,0:T(8,128)}, f32[2,1792,256]{2,1,0:T(8,128)}, bf16[2,2,1792,256]{3,2,1,0:T(8,128)(2,1)}) custom-call(s32[32]{0:T(128)} %slot_ref.3, s32[16]{0:T(128)} %owner_ref.1, bf16[6,1792,256]{2,1,0:T(8,128)(2,1)} %get-tuple-element.10.here_ref, bf16[2,1792,256]{2,1,0:T(8,128)(2,1)} %get-tuple-element.11.there_ref), custom_call_target="tpu_custom_call" | custom-call | tf_op jit(solution)/shard_map/expand/pallas_call | solution.py:277

commit v2 on v1

v2 whole, which is shorter than its diff:
```python
import functools

import jax
import jax.numpy as jnp
from jax import lax
from jax.experimental import pallas as pl
from jax.experimental.pallas import tpu as pltpu
from jax.sharding import PartitionSpec as P

beta_one = 0.9
beta_two = 0.95
learn_rate = 0.05
decay_rate = 0.1
adam_eps = 1e-08

MESH = pl.DeviceIdType.MESH
SIDE = 4
PEERS = SIDE * SIDE
FIELDS = 5
RESULTS = 6
PIECE = 16
ORDER = (
    (0, 1), (0, 3), (1, 0), (3, 0), (1, 1), (3, 3), (1, 3), (3, 1),
    (0, 2), (2, 0), (2, 1), (2, 3), (1, 2), (3, 2), (2, 2),
)


def exchange_kernel(
    chunks,
    old_hbm, slot_hbm, owner_hbm, count_hbm,
    master_ref, moment_ref, second_ref, grad_ref,
    out_ref, other_ref,
    *scratch,
):
    landed = scratch[:chunks]
    (states, grad_own, grad_other, packed, updated, table,
     old_ref, slot_ref, owner_ref, count_ref, table_sem,
     load_sem, dp_send, dp_recv, send_one, recv_one, send_two, recv_two,
     fwd_send, fwd_recv) = scratch[chunks:]
    tables = [
        pltpu.make_async_copy(source, held, table_sem.at[n])
        for n, (source, held) in enumerate(
            ((old_hbm, old_ref), (slot_hbm, slot_ref), (owner_hbm, owner_ref), (count_hbm, count_ref))
        )
    ]
    rows = states.shape[2]
    half = chunks * rows
    core = lax.axis_index("dp")
    me = lax.axis_index("expert")
    plane = lax.axis_index("etp")
    my_x = me // SIDE
    my_z = me % SIDE
    partner = (1 - core, me, plane)
    targets = [
        lax.rem(my_x + dx, SIDE) * SIDE + lax.rem(my_z + dz, SIDE) for dx, dz in ORDER
    ]

    def load_states(k):
        window = pl.ds(k * rows, rows)
        return [
            pltpu.make_async_copy(ref.at[0, window], states.at[k, a], load_sem.at[k, a])
            for a, ref in enumerate((master_ref, moment_ref, second_ref))
        ]

    def load_grads(k):
        return pltpu.make_async_copy(
            grad_ref.at[0, :, pl.ds(core * half + k * rows, rows)],
            grad_own.at[k],
            load_sem.at[k, 3],
        )

    def swap(k):
        return pltpu.make_async_remote_copy(
            src_ref=grad_ref.at[0, :, pl.ds((1 - core) * half + k * rows, rows)],
            dst_ref=grad_other.at[k],
            send_sem=dp_send.at[k],
            recv_sem=dp_recv.at[k],
            device_id=partner,
            device_id_type=MESH,
        )

    def spread(source, target, send, recv):
        for other in targets:
            pltpu.make_async_remote_copy(
                src_ref=source(other),
                dst_ref=target,
                send_sem=send,
                recv_sem=recv,
                device_id=(core, other, plane),
                device_id_type=MESH,
            ).start()
        pltpu.make_async_copy(source(me), target, recv).start()

    def scatter(k, first, count):
        spread(
            lambda i: packed.at[k, i, pl.ds(first, count)],
            landed[k].at[pl.ds(me * FIELDS + first, count)],
            send_one.at[k],
            recv_one.at[k],
        )

    def deliver(k, first, count, part):
        window = pl.ds(k * rows + me * PIECE, PIECE)
        spread(
            lambda i: updated.at[k, i, pl.ds(first, count)],
            out_ref.at[pl.ds(first, count), window],
            send_two.at[k],
            recv_two.at[k, part],
        )

    def pack_states(k):
        for copy in load_states(k):
            copy.wait()

        def body(i, carry):
            window = pl.ds(pl.multiple_of(i * PIECE, PIECE), PIECE)
            for a in range(3):
                packed[k, i, a] = states[k, a, window].astype(jnp.bfloat16)
            return carry

        lax.fori_loop(0, PEERS, body, 0)

    def pack_grads(k):
        load_grads(k).wait()
        swap(k).wait_recv()

        def body(i, carry):
            window = pl.ds(pl.multiple_of(i * PIECE, PIECE), PIECE)
            for h in range(2):
                packed[k, i, 3 + h] = (
                    grad_own[k, h, window].astype(jnp.float32)
                    + grad_other[k, h, window].astype(jnp.float32)
                ).astype(jnp.bfloat16)
            return carry

        lax.fori_loop(0, PEERS, body, 0)

    def update(k):
        source = landed[k]

        def body(d, carry):
            for h in range(2):
                s = 2 * d + h
                state = table[0, s]
                first = table[1, s]
                last = table[2, s]
                twice = table[3, s].astype(jnp.float32)
                scale = 1.0 / jnp.full((PIECE, 256), table[4, s].astype(jnp.float32))
                gradient = (
                    source[first].astype(jnp.float32)
                    + twice * source[last].astype(jnp.float32)
                ) * scale
                master = source[state].astype(jnp.float32)
                moment = source[state + 1].astype(jnp.float32)
                second = source[state + 2].astype(jnp.float32)
                moment = beta_one * moment + (1.0 - beta_one) * gradient
                second = beta_two * second + (1.0 - beta_two) * gradient * gradient
                master = master - learn_rate * (
                    moment / (jnp.sqrt(second) + adam_eps) + decay_rate * master
                )
                held = table[5, s] > 0
                owned = table[6, s] > 0
                updated[k, d, h] = jnp.where(held, master, 0.0).astype(jnp.bfloat16)
                updated[k, d, 2 + h] = jnp.where(owned, moment, 0.0).astype(jnp.bfloat16)
                updated[k, d, 4 + h] = jnp.where(owned, second, 0.0).astype(jnp.bfloat16)
            return carry

        lax.fori_loop(0, PEERS, body, 0)

    def forward(k):
        window = pl.ds(k * rows, rows)
        return pltpu.make_async_remote_copy(
            src_ref=out_ref.at[pl.ds(0, 2), window],
            dst_ref=other_ref.at[:, window],
            send_sem=fwd_send.at[k],
            recv_sem=fwd_recv.at[k],
            device_id=partner,
            device_id_type=MESH,
        )

    def all_bytes(ref, sem):
        pltpu.make_async_copy(ref, ref, sem).wait()

    for copy in tables:
        copy.start()
    for k in range(chunks):
        for copy in load_states(k) + [load_grads(k)]:
            copy.start()

    barrier = pltpu.get_barrier_semaphore()
    for other in targets:
        pl.semaphore_signal(
            barrier, inc=1, device_id=(core, other, plane), device_id_type=MESH
        )
    pl.semaphore_signal(barrier, inc=1, device_id=partner, device_id_type=MESH)
    pack_states(0)
    pl.semaphore_wait(barrier, PEERS)

    for k in range(chunks):
        swap(k).start()

    def fill_table(s, carry):
        expert = jnp.maximum(slot_ref[s], 0)
        holder = jnp.int32(0)
        for j in range(PEERS):
            holder = jnp.where(old_ref[j] == expert, j, holder)
        first = jnp.int32(0)
        last = jnp.int32(0)
        for t in range(2 * PEERS):
            last = jnp.where(slot_ref[t] == expert, t, last)
            back = 2 * PEERS - 1 - t
            first = jnp.where(slot_ref[back] == expert, back, first)
        table[0, s] = holder * FIELDS
        table[1, s] = (first // 2) * FIELDS + 3 + first % 2
        table[2, s] = (last // 2) * FIELDS + 3 + last % 2
        table[3, s] = jnp.where(first == last, 0, 1)
        table[4, s] = count_ref[expert]
        table[5, s] = jnp.where(slot_ref[s] >= 0, 1, 0)
        table[6, s] = jnp.where((slot_ref[s] >= 0) & (owner_ref[expert] == s), 1, 0)
        return carry

    scatter(0, 0, 3)
    pack_grads(0)
    scatter(0, 3, 2)
    pack_states(1)
    pack_grads(1)
    scatter(1, 0, FIELDS)
    for copy in tables:
        copy.wait()
    lax.fori_loop(0, 2 * PEERS, fill_table, 0)
    final = chunks - 1
    for k in range(chunks):
        all_bytes(landed[k], recv_one.at[k])
        update(k)
        if k < final:
            deliver(k, 0, RESULTS, 0)
        else:
            deliver(k, 0, 2, 0)
            deliver(k, 2, 4, 1)
        if k + 2 < chunks:
            pack_states(k + 2)
            pack_grads(k + 2)
            scatter(k + 2, 0, FIELDS)
    for k in range(chunks):
        fields = pl.ds(0, RESULTS if k < final else 2)
        all_bytes(out_ref.at[fields, pl.ds(k * rows, rows)], recv_two.at[k, 0])
        forward(k).start()
    all_bytes(out_ref.at[pl.ds(2, 4), pl.ds(final * rows, rows)], recv_two.at[final, 1])
    for k in range(chunks):
        swap(k).wait_send()
        all_bytes(packed.at[k, pl.ds(0, PEERS - 1)], send_one.at[k])
        all_bytes(updated.at[k, pl.ds(0, PEERS - 1)], send_two.at[k])
    for k in range(chunks):
        forward(k).wait()


def expand_kernel(
    slot_hbm, owner_hbm, here_ref, there_ref,
    master_ref, moment_ref, second_ref, weight_ref,
    wide, slot_ref, owner_ref, sems, weight_sems, table_sems,
):
    core = lax.axis_index("dp")
    me = lax.axis_index("expert")
    half = here_ref.shape[1]
    steps, rows = wide.shape[1], wide.shape[3]
    outs = (master_ref, moment_ref, second_ref)
    weights = [
        pltpu.make_async_copy(
            here_ref.at[pl.ds(0, 2)], weight_ref.at[:, pl.ds(core * half, half)], weight_sems.at[0]
        ),
        pltpu.make_async_copy(
            there_ref, weight_ref.at[:, pl.ds((1 - core) * half, half)], weight_sems.at[1]
        ),
    ]

    def store(a, k):
        return pltpu.make_async_copy(
            wide.at[a, k], outs[a].at[:, pl.ds(k * rows, rows)], sems.at[a, k]
        )

    tables = [
        pltpu.make_async_copy(slot_hbm, slot_ref, table_sems.at[0]),
        pltpu.make_async_copy(owner_hbm, owner_ref, table_sems.at[1]),
    ]
    for copy in tables + weights:
        copy.start()
    for a in (1, 2):
        for k in range(steps):
            for h in range(2):
                wide[a, k, h] = here_ref[2 * a + h, pl.ds(k * rows, rows)].astype(jnp.float32)
            store(a, k).start()
    for copy in tables:
        copy.wait()
    owned = []
    for h in range(2):
        slot = 2 * me + h
        expert = slot_ref[slot]
        owned.append((expert >= 0) & (owner_ref[jnp.maximum(expert, 0)] == slot))
    for k in range(steps):
        for h in range(2):
            value = here_ref[h, pl.ds(k * rows, rows)].astype(jnp.float32)
            wide[0, k, h] = jnp.where(owned[h], value, 0.0)
        store(0, k).start()
    for copy in weights:
        copy.wait()
    for k in range(steps):
        for a in range(3):
            store(a, k).wait()


def per_device(
    master_old, moment_old, second_old, grad_parts, old_expert, slot_expert, owner_slot, token_count
):
    half, width = master_old.shape[1:]
    rows = PEERS * PIECE
    chunks = half // rows
    anywhere = pl.BlockSpec(memory_space=pl.ANY)
    vmem = pl.BlockSpec(memory_space=pltpu.VMEM)
    bf16 = jnp.bfloat16
    dma = pltpu.SemaphoreType.DMA
    here, there = pl.pallas_call(
        functools.partial(exchange_kernel, chunks),
        out_shape=(
            pltpu.VMEM((RESULTS, half, width), bf16),
            pltpu.VMEM((2, half, width), bf16),
        ),
        in_specs=[anywhere] * 8,
        out_specs=(vmem, vmem),
        scratch_shapes=[pltpu.VMEM((PEERS * FIELDS, PIECE, width), bf16)] * chunks
        + [
            pltpu.VMEM((chunks, 3, rows, width), jnp.float32),
            pltpu.VMEM((chunks, 2, rows, width), bf16),
            pltpu.VMEM((chunks, 2, rows, width), bf16),
            pltpu.VMEM((chunks, PEERS, FIELDS, PIECE, width), bf16),
            pltpu.VMEM((chunks, PEERS, RESULTS, PIECE, width), bf16),
            pltpu.SMEM((7, 2 * PEERS), jnp.int32),
            pltpu.SMEM(old_expert.shape, jnp.int32),
            pltpu.SMEM(slot_expert.shape, jnp.int32),
            pltpu.SMEM(owner_slot.shape, jnp.int32),
            pltpu.SMEM(token_count.shape, jnp.int32),
            dma((4,)),
            dma((chunks, 4)),
            dma((chunks,)),
            dma((chunks,)),
            dma((chunks,)),
            dma((chunks,)),
            dma((chunks,)),
            dma((chunks, 2)),
            dma((chunks,)),
            dma((chunks,)),
        ],
        compiler_params=pltpu.CompilerParams(
            collective_id=0, has_side_effects=True, vmem_limit_bytes=40 << 20
        ),
        name="exchange",
    )(
        *(
            pltpu.with_memory_space_constraint(a, pltpu.HBM)
            for a in (
                old_expert, slot_expert, owner_slot, token_count,
                master_old, moment_old, second_old, grad_parts,
            )
        ),
    )

    steps = 7
    wide = jax.ShapeDtypeStruct((2, half, width), jnp.float32)
    return pl.pallas_call(
        expand_kernel,
        out_shape=(wide, wide, wide, jax.ShapeDtypeStruct((2, 2 * half, width), bf16)),
        in_specs=[anywhere, anywhere, vmem, vmem],
        out_specs=(anywhere,) * 4,
        scratch_shapes=[
            pltpu.VMEM((3, steps, 2, half // steps, width), jnp.float32),
            pltpu.SMEM(slot_expert.shape, jnp.int32),
            pltpu.SMEM(owner_slot.shape, jnp.int32),
            dma((3, steps)),
            dma((2,)),
            dma((2,)),
        ],
        compiler_params=pltpu.CompilerParams(vmem_limit_bytes=24 << 20),
        name="expand",
    )(
        pltpu.with_memory_space_constraint(slot_expert, pltpu.HBM),
        pltpu.with_memory_space_constraint(owner_slot, pltpu.HBM),
        here,
        there,
    )


def solution(mesh):
    placed = (
        P("expert", "dp", "etp"),
        P("expert", "dp", "etp"),
        P("expert", "dp", "etp"),
        P("dp", "expert", None, "etp"),
        P(),
        P(),
        P(),
        P(),
    )
    return jax.shard_map(
        per_device,
        mesh=mesh,
        in_specs=placed,
        out_specs=(
            P("expert", "dp", "etp"),
            P("expert", "dp", "etp"),
            P("expert", "dp", "etp"),
            P("expert", None, "etp"),
        ),
        check_vma=False,
    )
```

time: 135 us -> 125 us (0.926)
  Pallas kernels: 134 us -> 123 us
    pallas_call x1, Pallas kernels: 124 us -> 118 us  [per_device(): pl.pallas_call(functools.partial(exchange_kernel, chunks), out_shape=(plt...]
    pallas_call x1, Pallas kernels: 9.39 us -> 5.43 us  [per_device(): pl.pallas_call(expand_kernel, out_shape=(wide, wide, wide, jax.ShapeDtype...]
where the time goes in v2:
time: 125 us; the launch traced here: 124 us
  Pallas kernels  123 us (98%)
    pallas_call x1, Pallas kernels, per_device(): pl.pallas_call(functools.partial(exchange_kernel, chunks), out_shape=(plt...  118 us
    pallas_call x1, Pallas kernels, per_device(): pl.pallas_call(expand_kernel, out_shape=(wide, wide, wide, jax.ShapeDtype...  5.43 us

profile of v2, /device:TPU:1, one launch (start us, length us, event | category | flops | bytes accessed | tf_op | source)
XLA Modules:
  0.0 124.1 jit_solution(5011053826054386290)
XLA Ops:
  0.6 118.0 %exchange.1 = (bf16[6,1792,256]{2,1,0:T(8,128)(2,1)S(1)}, bf16[2,1792,256]{2,1,0:T(8,128)(2,1)S(1)}) custom-call(s32[16]{0:T(128)} %old_hbm.1, s32[32]{0:T(128)} %slot_hbm.3, s32[16]{0:T(128)} %owner_hbm.3, s32[16]{0:T(128)} %count_hbm.1, f32[1,1792,256]{2,1,0:T(8,128)} %master_ref.1, f32[1,1792,256]{2,1,0:T(8,128)} %moment_ref.1, ...), custom_call_target="tpu_custom_call" | custom-call | tf_op jit(solution)/shard_map/exchange/pallas_call | solution.py:321
  118.7 5.4 %expand.1 = (f32[2,1792,256]{2,1,0:T(8,128)}, f32[2,1792,256]{2,1,0:T(8,128)}, f32[2,1792,256]{2,1,0:T(8,128)}, bf16[2,3584,256]{2,1,0:T(8,128)(2,1)}) custom-call(s32[32]{0:T(128)} %slot_hbm.3, s32[16]{0:T(128)} %owner_hbm.3, bf16[6,1792,256]{2,1,0:T(8,128)(2,1)S(1)} %get-tuple-element.6.here_ref, bf16[2,1792,256]{2,1,0:T(8,128)(2,1)S(1)} %get-tuple-element.7.there_ref), custom_call_target="tpu_custom_call" | custom-call | tf_op jit(solution)/shard_map/expand/pallas_call | solution.py:368
